TPU v7x, 32 devices: a whole 2x2x4 slice. The times are simulated.
32 devices in a mesh: atom: 16 (over z, y, x), wave: 2 (over core).
Axes of the slice: x: 2, y: 2, z: 4, core: 2. Of those that a mesh axis runs over, the one named last changes fastest.
Arguments:
- positions: float32 [3, 4096], P(None, ('atom', 'wave')), may hold values from 0 to 1
- counts: int32 [32], P(('atom', 'wave')), may hold values from 16 to 128, as said below
- feats: bfloat16 [4096, 256], P(('atom', 'wave')), may hold values from -6 to 6
- waves: int32 [3, 8192], P(None, 'wave'), may hold values from -12 to 12
- wave_filter: bfloat16 [8192, 256], P('wave'), may hold values from -5 to 5
- mixing: float32 [256, 256], replicated, may hold values from -0.375 to 0.375
- gain: float32 [256], replicated, may hold values from 0.1 to 1.9
- w_in: bfloat16 [256, 1024], replicated, may hold values from -0.375 to 0.375
- w_out: bfloat16 [1024, 256], replicated, may hold values from -0.1875 to 0.1875
Outputs:
- updated: bfloat16 [4096, 256], P(('atom', 'wave'))
Inputs may be any that keep to these rules, and one draw needn't show every extreme that they name: `counts`: each block of 128 slots holds 16 to 128 live atoms at its start; every even-numbered block is full.
All inputs are finite; a program needn't handle non-finite values.
Results may differ from a plain program's by a relative error of at most 0.0055.
Values may be sent and summed in bfloat16 or wider, within the bound.
A program may use at most 128 MiB of HBM per device.

v0:
```python
import math

import jax
import jax.numpy as jnp
from jax import lax
from jax.sharding import PartitionSpec as P

two_pi = 2.0 * math.pi


def phases(coords, wave_f):
    return (
        coords[:, 0:1] * wave_f[0][None, :]
        + coords[:, 1:2] * wave_f[1][None, :]
        + coords[:, 2:3] * wave_f[2][None, :]
    ) * two_pi


def tiles(coords, wave_f):
    angle = phases(coords, wave_f)
    return (jnp.cos(angle).astype(jnp.bfloat16), jnp.sin(angle).astype(jnp.bfloat16))


def left_dot(tile, rows_h):
    return lax.dot_general(
        tile, rows_h, (((0,), (0,)), ((), ())), preferred_element_type=jnp.float32
    )


def body(positions, counts, feats, waves, wave_filter, mixing, gain, w_in, w_out):
    rows = feats.shape[0]
    width = feats.shape[1]
    live = (lax.broadcasted_iota(jnp.int32, (rows // 128, 128), 1) < counts[:, None]).reshape(rows)
    masked = feats * live[:, None].astype(jnp.bfloat16)
    coords = positions.T
    block_h = lax.all_gather(masked, "wave", axis=0, tiled=True)
    block_c = lax.all_gather(coords, "wave", axis=0, tiled=True)
    wave_f = waves.astype(jnp.float32)
    total = block_h.shape[0]
    size = math.gcd(total, 512)
    kw = waves.shape[1]
    atoms_all = rows * lax.axis_size("atom") * lax.axis_size("wave")
    kwaves_all = kw * lax.axis_size("wave")

    def forward(carry, index):
        cosine, sine = tiles(block_c, wave_f)
        return ((carry[0] + left_dot(cosine, block_h), carry[1] + left_dot(sine, block_h)), None)

    zero = jnp.zeros((kw, width), jnp.float32)
    (part_real, part_imag), _ = lax.scan(
        forward, (zero, zero), jnp.arange(total // size, dtype=jnp.int32)
    )
    scale = 1.0 / math.sqrt(atoms_all)

    def filter_mix(summed, filt):
        return jnp.dot(summed * scale * filt, mixing, precision=lax.Precision.HIGHEST).astype(
            jnp.bfloat16
        )

    sum_real, sum_imag = lax.psum((part_real, part_imag), "atom")
    filt = wave_filter.astype(jnp.float32)
    filtered_real = filter_mix(sum_real, filt)
    filtered_imag = filter_mix(sum_imag, filt)
    inv_k = 1.0 / math.sqrt(kwaves_all)
    step = math.gcd(rows * lax.axis_size("wave"), 512)

    def one_block(index):
        cosine, sine = tiles(block_c, wave_f)
        field = jnp.dot(cosine, filtered_real, preferred_element_type=jnp.float32) + jnp.dot(
            sine, filtered_imag, preferred_element_type=jnp.float32
        )
        return field * inv_k

    update = lax.psum_scatter(
        lax.map(
            one_block, jnp.arange(rows * lax.axis_size("wave") // step, dtype=jnp.int32)
        ).reshape(rows * lax.axis_size("wave"), width),
        "wave",
        scatter_dimension=0,
        tiled=True,
    )
    state = feats.astype(jnp.float32) + update
    meansq = jnp.mean(state * state, axis=1, keepdims=True)
    normed = (state * lax.rsqrt(meansq + 1e-06) * gain[None, :]).astype(jnp.bfloat16)
    hidden = jax.nn.silu(jnp.dot(normed, w_in, preferred_element_type=jnp.float32)).astype(
        jnp.bfloat16
    )
    result = state + jnp.dot(hidden, w_out, preferred_element_type=jnp.float32)
    return jnp.where(live[:, None], result, 0.0).astype(jnp.bfloat16)


def solution(mesh):
    return jax.shard_map(
        body,
        mesh=mesh,
        in_specs=(
            P(None, ("atom", "wave")),
            P(("atom", "wave")),
            P(("atom", "wave"), None),
            P(None, "wave"),
            P("wave", None),
            P(),
            P(),
            P(),
            P(),
        ),
        out_specs=P(("atom", "wave"), None),
        check_vma=False,
    )
```

profile of v0, /device:TPU:0, one launch (start us, length us, event | category | flops | bytes accessed | tf_op | source)
XLA Modules:
  0.0 364.1 jit_solution(7670962397245622199)
XLA Ops:
  6.5 0.0 copy-start
  6.5 0.0 all-reduce.3.cloned.1.call-start
  7.3 2.1 all_gather.6
  9.4 0.9 broadcast_multiply_fusion
  10.3 1.9 all_gather.7
  12.2 0.9 convert_element_type.45
  13.1 16.4 %fusion.7 = f32[4096,256]{1,0:T(8,128)} fusion(bf16[256,256]{1,0:T(8,128)(2,1)S(1)} %all_gather.7, f32[4096]{0:T(1024)S(1)} %bitcast.22, f32[256]{0:T(256)S(1)} %bitcast.35, f32[4096]{0:T(1024)S(1)} %bitcast.26, f32[256]{0:T(256)S(1)} %bitcast.39, f32[4096]{0:T(1024)S(1)} %bitcast.18, f32[256]{0:T(256)S(1)} %bitcast.31), kind=kOutput, calls=%fused_computation.14 | convolution fusion | flops 544210944 | bytes 4377600 | tf_op jit(solution)/shard_map/while/body/eval_jaxpr/dot_general | solution.py:25
  29.5 16.4 %fusion.5 = f32[4096,256]{1,0:T(8,128)} fusion(bf16[256,256]{1,0:T(8,128)(2,1)S(1)} %all_gather.7, f32[4096]{0:T(1024)S(1)} %bitcast.23, f32[256]{0:T(256)S(1)} %bitcast.36, f32[4096]{0:T(1024)S(1)} %bitcast.27, f32[256]{0:T(256)S(1)} %bitcast.40, f32[4096]{0:T(1024)S(1)} %bitcast.19, f32[256]{0:T(256)S(1)} %bitcast.32), kind=kOutput, calls=%fused_computation.12 | convolution fusion | flops 544210944 | bytes 4377600 | tf_op jit(solution)/shard_map/while/body/eval_jaxpr/dot_general | solution.py:25
  45.9 0.0 copy-start.1
  45.9 0.0 copy-start.3
  45.9 0.0 all-reduce.3.cloned.1.call-update
  46.0 0.0 reduce-scatter.2.cloned.1.call-start
  46.0 258.4 %all-reduce.3.cloned.1.call-done = (f32[4096,256]{1,0:T(8,128)}, f32[4096,256]{1,0:T(8,128)}) async-done(((f32[4096,256]{1,0:T(8,128)}, f32[4096,256]{1,0:T(8,128)}), (f32[4096,256]{1,0:T(8,128)}, f32[4096,256]{1,0:T(8,128)})) %all-reduce.3.cloned.1.call-update) | async-done | bytes 8388624 | tf_op jit(solution)/shard_map/psum | solution.py:60
  304.4 0.0 copy-done.1
  304.4 0.0 copy-done.3
  304.4 0.0 copy-start.2
  304.4 5.8 %convolution_convert_fusion.1 = bf16[4096,256]{1,0:T(8,128)(2,1)S(1)} fusion(f32[256,256]{1,0:T(8,128)S(1)} %copy-done.3, bf16[4096,256]{1,0:T(8,128)(2,1)S(1)} %copy-done.1, f32[4096,256]{1,0:T(8,128)} %get-tuple-element.27), kind=kOutput, calls=%fused_computation.3 | convolution fusion | flops 3225419776 | bytes 8650752 | tf_op jit(solution)/shard_map/dot_general | solution.py:56
  310.2 0.0 copy-done.2
  310.2 4.1 %convolution_convert_fusion = bf16[4096,256]{1,0:T(8,128)(2,1)S(1)} fusion(f32[256,256]{1,0:T(8,128)S(1)} %copy-done.3, bf16[4096,256]{1,0:T(8,128)(2,1)S(1)} %copy-done.1, f32[4096,256]{1,0:T(8,128)S(1)} %copy-done.2), kind=kOutput, calls=%fused_computation.2 | convolution fusion | flops 3225419776 | bytes 8650752 | tf_op jit(solution)/shard_map/dot_general | solution.py:56
  314.3 15.8 %fusion.4 = f32[256,256]{1,0:T(8,128)S(1)} fusion(bf16[4096,256]{1,0:T(8,128)(2,1)S(1)} %convolution_convert_fusion.1, f32[4096]{0:T(1024)S(1)} %bitcast.24, f32[256]{0:T(256)S(1)} %bitcast.37, f32[4096]{0:T(1024)S(1)} %bitcast.28, f32[256]{0:T(256)S(1)} %bitcast.41, f32[4096]{0:T(1024)S(1)} %bitcast.20, f32[256]{0:T(256)S(1)} %bitcast.33), kind=kOutput, calls=%fused_computation.11 | convolution fusion | flops 544210944 | bytes 2411520 | tf_op jit(solution)/shard_map/while/body/eval_jaxpr/dot_general | solution.py:69
  330.2 0.0 copy-start.4
  330.2 0.0 copy-start.5
  330.2 0.0 copy-start.6
  330.2 16.7 %fusion.9 = f32[256,256]{1,0:T(8,128)} fusion(f32[256,256]{1,0:T(8,128)S(1)} %fusion.4, bf16[4096,256]{1,0:T(8,128)(2,1)S(1)} %convolution_convert_fusion, f32[4096]{0:T(1024)S(1)} %bitcast.25, f32[256]{0:T(256)S(1)} %bitcast.38, f32[4096]{0:T(1024)S(1)} %bitcast.29, f32[256]{0:T(256)S(1)} %bitcast.42, f32[4096]{0:T(1024)S(1)} %bitcast.21, f32[256]{0:T(256)S(1)} %bitcast.34), kind=kOutput, calls=%fused_computation.16 | convolution fusion | flops 544342016 | bytes 2673664 | tf_op jit(solution)/shard_map/while/body/eval_jaxpr/dot_general | solution.py:69
  346.9 0.0 reduce-scatter.2.cloned.1.call-update
  347.0 6.9 %reduce-scatter.2.cloned.1.call-done = f32[128,256]{1,0:T(8,128)} async-done(((f32[256,256]{1,0:T(8,128)}), f32[128,256]{1,0:T(8,128)}) %reduce-scatter.2.cloned.1.call-update) | async-done | bytes 131088 | tf_op jit(solution)/shard_map/reduce_scatter | solution.py:74
  353.9 0.0 copy-done.4
  353.9 1.0 multiply_reduce_fusion
  354.9 0.0 copy-done
  354.9 0.0 copy-done.5
  355.0 0.0 copy-done.6
  355.0 2.1 fusion.11
  (5 shorter events, 0.1 us)
Async XLA Ops:
  6.5 348.4 %copy-start = (bf16[1024,256]{1,0:T(8,128)(2,1)S(1)}, bf16[1024,256]{1,0:T(8,128)(2,1)}, u32[]{:S(2)}) copy-start(bf16[1024,256]{1,0:T(8,128)(2,1)} %param.17) | copy-start | bytes 1572868
  6.5 297.9 %all-reduce.3.cloned.1.call-start = ((), (), s32[]{:S(2)}) async-start(), calls=%async_computation.2 | async-start | bytes 16777216 | tf_op jit(solution)/shard_map/psum | solution.py:60
  45.9 258.5 %copy-start.1 = (bf16[4096,256]{1,0:T(8,128)(2,1)S(1)}, bf16[4096,256]{1,0:T(8,128)(2,1)}, u32[]{:S(2)}) copy-start(bf16[4096,256]{1,0:T(8,128)(2,1)} %param.13) | copy-start | bytes 6291460
  45.9 258.5 %copy-start.3 = (f32[256,256]{1,0:T(8,128)S(1)}, f32[256,256]{1,0:T(8,128)}, u32[]{:S(2)}) copy-start(f32[256,256]{1,0:T(8,128)} %param.14) | copy-start | bytes 786436
  46.0 307.9 %reduce-scatter.2.cloned.1.call-start = ((), (), s32[]{:S(2)}) async-start(), calls=%async_computation.1 | async-start | bytes 393216 | tf_op jit(solution)/shard_map/reduce_scatter | solution.py:74
  304.4 5.8 %copy-start.2 = (f32[4096,256]{1,0:T(8,128)S(1)}, f32[4096,256]{1,0:T(8,128)}, u32[]{:S(2)}) copy-start(f32[4096,256]{1,0:T(8,128)} %get-tuple-element.28) | copy-start | bytes 12582916
  330.2 23.7 %copy-start.4 = (bf16[128,256]{1,0:T(8,128)(2,1)S(1)}, bf16[128,256]{1,0:T(8,128)(2,1)}, u32[]{:S(2)}) copy-start(bf16[128,256]{1,0:T(8,128)(2,1)} %param.11) | copy-start | bytes 196612
  330.2 24.8 %copy-start.5 = (bf16[256,1024]{1,0:T(8,128)(2,1)S(1)}, bf16[256,1024]{1,0:T(8,128)(2,1)}, u32[]{:S(2)}) copy-start(bf16[256,1024]{1,0:T(8,128)(2,1)} %param.16) | copy-start | bytes 1572868
  330.2 24.8 %copy-start.6 = (f32[256]{0:T(256)S(1)}, f32[256]{0:T(256)}, u32[]{:S(2)}) copy-start(f32[256]{0:T(256)} %param.15) | copy-start | bytes 3076
Sparse Core Ops, SparseCore 0:
  46.1 258.2 all-reduce.2
  347.1 6.7 reduce-scatter.1
where the time goes:
time: 370 us; the launch traced here: 364 us
  waiting for transfers between devices  265 us (72%)
  matrix products  77.3 us (21%)
  between operations  14.5 us (4%)
  blocking collectives  4.02 us (1%)
    psum x1, waiting for transfers between devices, body(): sum_real, sum_imag = lax.psum((part_real, part_imag), 'atom')  258 us
    dot_general x2, matrix products, left_dot(): lax.dot_general(tile, rows_h, (((0,), (0,)), ((), ())), preferred_element...  32.8 us
    dot_general x1, matrix products, one_block(): jnp.dot(sine, filtered_imag, preferred_element_type=jnp.float32)  16.7 us
    dot_general x1, matrix products, one_block(): jnp.dot(cosine, filtered_real, preferred_element_type=jnp.float32)  15.8 us
    dot_general x2, matrix products, filter_mix(): jnp.dot(summed * scale * filt, mixing, precision=lax.Precision.HIGHEST)  9.9 us
  transfers between devices with their start and end apart: 2, of which 2 were waited for; matrix products, arithmetic and copies ran while one was open for 0% of the time, Pallas kernels for 0%

commit v1 on v0

v1 whole, which is shorter than its diff:
```python
import functools
import math

import jax
import jax.numpy as jnp
from jax import lax
from jax.experimental import pallas as pl
from jax.experimental.pallas import tpu as pltpu
from jax.sharding import PartitionSpec as P

MESH = pl.DeviceIdType.MESH
BF, F32 = jnp.bfloat16, jnp.float32
HIGHEST = lax.Precision.HIGHEST
SIN = (4.442883014678955, -7.308245658874512, 3.606354236602783, -0.8461116552352905, 0.1098245158791542)
COS = (1.4142135381698608, -6.978850841522217, 5.739460468292236, -1.883557915687561, 0.3106880187988281)


def horner(z, coefs):
    total = coefs[-1]
    for value in coefs[-2::-1]:
        total = total * z + value
    return total


def grid_of(n):
    side = 1
    while n % (4 * side * side) == 0 and 8 * side**3 <= n:
        side *= 2
    return n // (side * side), side


def kernel(
    n,
    planes,
    side,
    atoms_all,
    kwaves_all,
    counts_ref,
    pos_ref,
    masked_ref,
    wave_ref,
    filt_ref,
    mixing_ref,
    gain_ref,
    w_in_ref,
    w_out_ref,
    out_ref,
    pos_all,
    feat_all,
    wave_other,
    trig,
    factors,
    factors_in,
    field_t,
    field_other,
    kept,
    send_u,
    recv_u,
    p_send,
    p_recv,
    f_send,
    f_recv,
    u_send,
    u_recv,
    c_send,
    c_recv,
):
    kw = wave_ref.shape[0]
    rows, width = masked_ref.shape
    me = lax.axis_index("atom")
    core = lax.axis_index("wave")
    x = me % side
    y = (me // side) % side
    z = me // (side * side)
    b = y + core * (x - y)
    c = x + core * (y - x)
    stride_b = side + core * (1 - side)
    stride_c = 1 + core * (side - 1)

    def at(zz, bb, cc):
        return (zz * (side * side) + bb * stride_b + cc * stride_c, core)

    def ident(dz, db, dc):
        return (dc * side + db) * planes + dz

    partner = (me, 1 - core)
    ahead = (
        [at((z + d) % planes, b, c) for d in range(1, planes)],
        [at(z, (b + d) % side, c) for d in range(1, side)],
        [at(z, b, (c + d) % side) for d in range(1, side)],
    )
    back = (
        [at((z + planes - d) % planes, b, c) for d in range(1, planes)],
        [at(z, (b + side - d) % side, c) for d in range(1, side)],
        [at(z, b, (c + side - d) % side) for d in range(1, side)],
    )

    barrier = pltpu.get_barrier_semaphore()
    peers = [partner] + [peer for group in ahead for peer in group]
    for peer in peers:
        pl.semaphore_signal(barrier, inc=1, device_id=peer, device_id_type=MESH)
    pl.semaphore_wait(barrier, len(peers))

    def gather(own, store, send, recv):
        def copy(src_id, dst_id, peer):
            src = own if src_id == 0 else store.at[src_id]
            return pltpu.make_async_remote_copy(
                src_ref=src,
                dst_ref=store.at[dst_id],
                send_sem=send.at[dst_id],
                recv_sem=recv.at[dst_id],
                device_id=peer,
                device_id_type=MESH,
            )

        copies = {}

        def start(src_id, dst_id, peer):
            copies[dst_id] = copy(src_id, dst_id, peer)
            copies[dst_id].start()

        def forward(dz, db):
            if db == 0:
                for d in range(1, side):
                    start(ident(dz, 0, 0), ident(dz, d, 0), ahead[1][d - 1])
            for d in range(1, side):
                start(ident(dz, db, 0), ident(dz, db, d), ahead[2][d - 1])

        def begin():
            for d in range(1, planes):
                start(0, d, ahead[0][d - 1])
            forward(0, 0)

        def arrive(dz, db, dc):
            copies[ident(dz, db, dc)].wait_recv()

        return begin, forward, arrive, copies

    p_begin, p_forward, p_arrive, p_copies = gather(pos_ref, pos_all, p_send, p_recv)
    f_begin, f_forward, f_arrive, f_copies = gather(masked_ref, feat_all, f_send, f_recv)

    def core_copy(src, dst, k):
        return pltpu.make_async_remote_copy(
            src_ref=src,
            dst_ref=dst,
            send_sem=c_send.at[k],
            recv_sem=c_recv.at[k],
            device_id=partner,
            device_id_type=MESH,
        )

    p_begin()
    wave_copy = core_copy(wave_ref, wave_other, 0)
    wave_copy.start()
    f_begin()
    pos_all[0] = pos_ref[...]
    feat_all[0] = masked_ref[...]
    mixing_t = mixing_ref[...].T
    wave_copy.wait_recv()

    block = min(kw, 128)

    def angles(dz, db, dc):
        k = ident(dz, db, dc)
        place = pos_all[k]
        columns = slice(k * rows, (k + 1) * rows)
        for half, ref in enumerate((wave_ref, wave_other)):

            def one(j, carry):
                r0 = pl.multiple_of(j * block, block)
                turns = jnp.dot(
                    ref[pl.ds(r0, block), :][:, :16], place, preferred_element_type=F32
                )
                r = turns - jnp.round(turns)
                zz = r * r
                s = r * horner(zz, SIN)
                co = horner(zz, COS)
                base = half * 2 * kw
                trig[pl.ds(base + r0, block), columns] = (1.0 - s * s).astype(BF)
                trig[pl.ds(base + kw + r0, block), columns] = (s * co).astype(BF)
                return carry

            lax.fori_loop(0, kw // block, one, 0)

    group_cols = planes * rows
    step = min(2 * kw, 256)

    def sums(g, lo, hi, first):
        columns = slice(g * group_cols, (g + 1) * group_cols)

        def one(j, carry):
            r0 = pl.multiple_of(lo + j * step, step)
            feats_g = feat_all[g * planes : (g + 1) * planes].reshape(group_cols, width)
            part = jnp.dot(
                trig[pl.ds(r0, step), columns], feats_g, preferred_element_type=F32
            )
            if first:
                factors[pl.ds(r0, step), :] = part
            else:
                factors[pl.ds(r0, step), :] += part
            return carry

        lax.fori_loop(0, (hi - lo) // step, one, 0)

    angles(0, 0, 0)
    for dz in range(1, planes):
        p_arrive(dz, 0, 0)
        p_forward(dz, 0)
    for dz in range(1, planes):
        angles(dz, 0, 0)
        f_arrive(dz, 0, 0)
        f_forward(dz, 0)
    for db in range(1, side):
        for dz in range(planes):
            p_arrive(dz, db, 0)
            p_forward(dz, db)
    for db in range(1, side):
        for dz in range(planes):
            angles(dz, db, 0)
            f_arrive(dz, db, 0)
            f_forward(dz, db)
    groups = side * side
    for g in range(side):
        if g < groups - 1:
            sums(g, 0, 4 * kw, g == 0)
    for dc in range(1, side):
        for db in range(side):
            for dz in range(planes):
                p_arrive(dz, db, dc)
                angles(dz, db, dc)
    for dc in range(1, side):
        for db in range(side):
            for dz in range(planes):
                f_arrive(dz, db, dc)
            g = dc * side + db
            if g < groups - 1:
                sums(g, 0, 4 * kw, False)
    last = groups - 1
    sums(last, 2 * kw, 4 * kw, last == 0)
    sum_copy = core_copy(factors.at[pl.ds(2 * kw, 2 * kw)], factors_in, 1)
    sum_copy.start()
    sums(last, 0, 2 * kw, last == 0)
    filt = filt_ref[...].astype(F32)
    scale = 1.0 / math.sqrt(atoms_all)
    sum_copy.wait_recv()
    for part in range(2):
        span = slice(part * kw, (part + 1) * kw)
        total = (factors[span, :] + factors_in[span, :]) * scale * filt
        field_t[:, span] = lax.dot_general(
            mixing_t, total, (((1,), (1,)), ((), ())), precision=HIGHEST,
            preferred_element_type=F32,
        ).astype(BF)
    field_copy = core_copy(field_t, field_other, 2)
    field_copy.start()
    field_copy.wait_recv()

    inv_k = 1.0 / math.sqrt(kwaves_all)

    def update_pair(k):
        columns = slice(k * rows, (k + 2) * rows)
        return jnp.dot(
            field_t[...], trig[: 2 * kw, columns], preferred_element_type=F32
        ) + jnp.dot(field_other[...], trig[2 * kw :, columns], preferred_element_type=F32)

    u_copies = {}

    def start_u(k, dst_id, peer):
        u_copies[dst_id] = pltpu.make_async_remote_copy(
            src_ref=send_u.at[k],
            dst_ref=recv_u.at[dst_id],
            send_sem=u_send.at[dst_id],
            recv_sem=u_recv.at[dst_id],
            device_id=peer,
            device_id_type=MESH,
        )
        u_copies[dst_id].start()

    def received(k):
        u_copies[k].wait_recv()
        return recv_u[k].astype(F32)

    order = [(dz, db) for db in range(side - 1, -1, -1) for dz in range(planes - 2, -1, -2)]
    for dz, db in order:
        for dc in range(1, side):
            k = ident(dz, db, dc)
            pair = update_pair(k)
            for d in range(2):
                send_u[k + d] = pair[:, d * rows : (d + 1) * rows].astype(BF)
                start_u(k + d, k + d, back[2][dc - 1])
    for dz, db in order:
        k = ident(dz, db, 0)
        pair = update_pair(k)
        for d in range(2):
            kept[k + d] = pair[:, d * rows : (d + 1) * rows]

    def collected(dz, db):
        acc = kept[ident(dz, db, 0)]
        for d in range(1, side):
            acc = acc + received(ident(dz, db, d))
        if db == 0:
            for d in range(1, side):
                acc = acc + received(ident(dz, d, 0))
        return acc

    zorder = [dz + d for dz in range(planes - 2, -1, -2) for d in range(2)]
    for db in range(side - 1, 0, -1):
        for dz in zorder:
            k = ident(dz, db, 0)
            send_u[k] = collected(dz, db).astype(BF)
            start_u(k, k, back[1][db - 1])
    for dz in zorder:
        if dz:
            send_u[dz] = collected(dz, 0).astype(BF)
            start_u(dz, dz, back[0][dz - 1])
    mine = collected(0, 0)
    for dz in range(1, planes):
        mine = mine + received(dz)

    state = masked_ref[...].astype(F32) + mine.T * inv_k
    meansq = jnp.mean(state * state, axis=1, keepdims=True)
    normed = (state * lax.rsqrt(meansq + 1e-06) * gain_ref[...]).astype(BF)
    inner = jnp.dot(normed, w_in_ref[...], preferred_element_type=F32)
    hidden = (inner / (1.0 + jnp.exp(-inner))).astype(BF)
    result = state + jnp.dot(hidden, w_out_ref[...], preferred_element_type=F32)
    slot = lax.broadcasted_iota(jnp.int32, (rows, width), 0)
    out_ref[...] = jnp.where(slot < counts_ref[0], result, 0.0).astype(BF)

    for copies in (p_copies, f_copies, u_copies):
        for copy in copies.values():
            copy.wait_send()
    for copy in (wave_copy, sum_copy, field_copy):
        copy.wait_send()


def body(n, cores, positions, counts, feats, waves, wave_filter, mixing, gain, w_in, w_out):
    rows, width = feats.shape
    planes, side = grid_of(n)
    kwaves_all = waves.shape[1] * cores
    kw = waves.shape[1] // n
    me = lax.axis_index("atom")
    live = lax.broadcasted_iota(jnp.int32, (rows, 1), 0) < counts[0]
    masked = feats * live.astype(BF)
    high = lax.reduce_precision(positions, 8, 7)
    rest = positions - high
    middle = lax.reduce_precision(rest, 8, 7)
    low = rest - middle
    pos = jnp.pad(jnp.concatenate([high, middle, low], 0).astype(BF), ((0, 7), (0, 0)))
    own = lax.dynamic_slice_in_dim(waves, me * kw, kw, 1).astype(BF).T
    wave = jnp.pad(jnp.concatenate([own, own, own], 1), ((0, 0), (0, 119)))
    filt = lax.dynamic_slice_in_dim(wave_filter, me * kw, kw, 0)
    vmem = pl.BlockSpec(memory_space=pltpu.VMEM)
    return pl.pallas_call(
        functools.partial(kernel, n, planes, side, rows * n * cores, kwaves_all),
        out_shape=jax.ShapeDtypeStruct((rows, width), BF),
        in_specs=[pl.BlockSpec(memory_space=pltpu.SMEM)] + [vmem] * 8,
        out_specs=vmem,
        scratch_shapes=[
            pltpu.VMEM((n, 16, rows), BF),
            pltpu.VMEM((n, rows, width), BF),
            pltpu.VMEM((kw, 128), BF),
            pltpu.VMEM((4 * kw, n * rows), BF),
            pltpu.VMEM((4 * kw, width), F32),
            pltpu.VMEM((2 * kw, width), F32),
            pltpu.VMEM((width, 2 * kw), BF),
            pltpu.VMEM((width, 2 * kw), BF),
            pltpu.VMEM((n // side, width, rows), F32),
            pltpu.VMEM((n, width, rows), BF),
            pltpu.VMEM((n, width, rows), BF),
        ]
        + [pltpu.SemaphoreType.DMA((n,))] * 6
        + [pltpu.SemaphoreType.DMA((3,))] * 2,
        compiler_params=pltpu.CompilerParams(
            collective_id=0, has_side_effects=True, vmem_limit_bytes=60 * 2**20
        ),
    )(counts, pos, masked, wave, filt, mixing, gain[None, :], w_in, w_out)


def solution(mesh):
    n, cores = mesh.shape["atom"], mesh.shape["wave"]
    return jax.shard_map(
        functools.partial(body, n, cores),
        mesh=mesh,
        in_specs=(
            P(None, ("atom", "wave")),
            P(("atom", "wave")),
            P(("atom", "wave"), None),
            P(None, "wave"),
            P("wave", None),
            P(),
            P(),
            P(),
            P(),
        ),
        out_specs=P(("atom", "wave"), None),
        check_vma=False,
    )
```

time: 370 us -> 56.9 us (0.15); the launches traced: 364 us -> 56.6 us
  waiting for transfers between devices: 265 us -> 0 us
  matrix products: 77.3 us -> 0 us
  Pallas kernels: 0 us -> 49.4 us
  between operations: 14.5 us -> 0.82 us
  blocking collectives: 4.02 us -> 0 us
    psum x1 -> x0, waiting for transfers between devices: 258 us -> none  [body(): sum_real, sum_imag = lax.psum((part_real, part_imag), 'atom')]
    dot_general x7 -> x0, matrix products: 77.3 us -> none  [the longest x2 32.8 us: left_dot(): lax.dot_general(tile, rows_h, (((0,), (0,)), ((), ())), preferred_element...]
    pallas_call x0 -> x1, Pallas kernels: none -> 49.4 us  [body(): pl.pallas_call(functools.partial(kernel, n, planes, side, rows * n * core...]
    reduce_scatter x1 -> x0, waiting for transfers between devices: 6.93 us -> none  [body(): lax.psum_scatter(lax.map(one_block, jnp.arange(rows * lax.axis_size('wave...]
    all_gather x2 -> x0, blocking collectives: 4.02 us -> none  [the longest x1 2.12 us: body(): block_c = lax.all_gather(coords, 'wave', axis=0, tiled=True)]
  transfers between devices with their start and end apart: 2 -> 0, of which waited for: 2 -> 0; matrix products, arithmetic and copies ran while one was open for 0% -> 0% of each run, Pallas kernels for 0% -> 0%
where the time goes in v1:
time: 56.9 us; the launch traced here: 56.6 us
  Pallas kernels  49.4 us (87%)
  other arithmetic  3.56 us (6%)
  local copies, waits for them, and re-layouts  2.89 us (5%)
  between operations  0.82 us (1%)
    pallas_call x1, Pallas kernels, body(): pl.pallas_call(functools.partial(kernel, n, planes, side, rows * n * core...  49.4 us
    mul x1, other arithmetic, body(): masked = feats * live.astype(BF)  1.55 us
    unnamed x3, local copies, waits for them, and re-layouts  1.48 us

profile of v1, /device:TPU:0, one launch (start us, length us, event | category | flops | bytes accessed | tf_op | source)
XLA Modules:
  0.0 56.6 jit_solution(17526579633658801911)
XLA Ops:
  0.0 0.0 copy-start
  0.8 0.7 %fusion.6 = bf16[256,3]{0,1:T(4,128)(2,1)S(1)} fusion(s32[3,4096]{1,0:T(4,128)} %param.12, s32[]{:T(128)S(6)} %select_n.4), kind=kLoop, calls=%fused_computation.14 | loop fusion | flops 768 | bytes 4612 | tf_op jit(solution)/shard_map/transpose | solution.py:348
  1.5 0.7 %reduce-precision_convert_fusion.1 = (bf16[3,128]{1,0:T(4,128)(2,1)S(1)}, bf16[3,128]{1,0:T(4,128)(2,1)S(1)}, bf16[3,128]{1,0:T(4,128)(2,1)S(1)}) fusion(f32[3,128]{1,0:T(4,128)} %param.9), kind=kLoop, calls=%fused_computation.12 | loop fusion | flops 2688 | bytes 3840 | tf_op jit(solution)/shard_map/convert
  2.2 0.6 %fusion.4.pos_ref = bf16[16,128]{1,0:T(8,128)(2,1)} fusion(bf16[3,128]{1,0:T(4,128)(2,1)S(1)} %get-tuple-element.6, bf16[3,128]{1,0:T(4,128)(2,1)S(1)} %get-tuple-element.7, bf16[3,128]{1,0:T(4,128)(2,1)S(1)} %get-tuple-element.5), kind=kLoop, calls=%fused_computation.7 | loop fusion | flops 20480 | bytes 6400 | tf_op jit(solution)/shard_map/concatenate | solution.py:347
  2.8 0.1 copy.11
  3.0 0.6 %pad.9.wave_ref = bf16[256,128]{1,0:T(8,128)(2,1)} pad(bf16[256,9]{1,0:T(8,128)(2,1)S(1)} %copy.11, bf16[]{:T(256)} %constant.3.clone.1), padding=0_0x0_119 | pad | bytes 70146 | tf_op jit(solution)/shard_map/jit(_pad)/pad | solution.py:349
  3.6 1.6 %broadcast_multiply_fusion.masked_ref = bf16[128,256]{1,0:T(8,128)(2,1)} fusion(bf16[128,256]{1,0:T(8,128)(2,1)} %param.11, bf16[128]{0:T(256)(128)(2,1)S(1)} %compare_convert_fusion), kind=kLoop, calls=%fused_computation | loop fusion | flops 32768 | bytes 131328 | tf_op jit(solution)/shard_map/mul | solution.py:342
  5.1 0.0 copy-done
  5.2 0.6 %constant_dynamic-slice_fusion.filt_ref = bf16[256,256]{1,0:T(8,128)(2,1)} fusion(bf16[4096,256]{1,0:T(8,128)(2,1)S(1)} %copy-done, s32[]{:T(128)S(6)} %select_n.4), kind=kLoop, calls=%fused_computation.16 | loop fusion | bytes 262148 | tf_op jit(solution)/shard_map/dynamic_slice | solution.py:350
  5.8 49.4 %shard_map.91 = bf16[128,256]{1,0:T(8,128)(2,1)} custom-call(s32[1]{0:T(128)} %copy.13.counts_ref, bf16[16,128]{1,0:T(8,128)(2,1)} %fusion.4.pos_ref, bf16[128,256]{1,0:T(8,128)(2,1)} %broadcast_multiply_fusion.masked_ref, bf16[256,128]{1,0:T(8,128)(2,1)} %pad.9.wave_ref, bf16[256,256]{1,0:T(8,128)(2,1)} %constant_dynamic-slice_fusion.filt_ref, ...), custom_call_target="tpu_custom_call" | custom-call | tf_op jit(solution)/shard_map/pallas_call | solution.py:352
  55.2 1.5 %copy.14 = bf16[128,256]{1,0:T(8,128)(2,1)} copy(bf16[128,256]{1,0:T(8,128)(2,1)} %shard_map.91) | data formatting | bytes 131072
  (2 shorter events, 0.0 us)
Async XLA Ops:
  0.0 5.1 %copy-start = (bf16[4096,256]{1,0:T(8,128)(2,1)S(1)}, bf16[4096,256]{1,0:T(8,128)(2,1)}, u32[]{:S(2)}) copy-start(bf16[4096,256]{1,0:T(8,128)(2,1)} %param.13) | copy-start | bytes 6291460

commit v2 on v1

--- a/solution.py
+++ b/solution.py
@@ -37,14 +37,21 @@
     kwaves_all,
     counts_ref,
     pos_ref,
-    masked_ref,
-    wave_ref,
+    feats_ref,
+    waves_ref,
+    filt_hbm,
+    mixing_hbm,
+    gain_ref,
+    w_in_hbm,
+    w_out_hbm,
+    out_ref,
     filt_ref,
     mixing_ref,
-    gain_ref,
     w_in_ref,
     w_out_ref,
-    out_ref,
+    stage,
+    wave_own,
+    wave_raw,
     pos_all,
     feat_all,
     wave_other,
@@ -64,9 +71,10 @@
     u_recv,
     c_send,
     c_recv,
+    l_sem,
 ):
-    kw = wave_ref.shape[0]
-    rows, width = masked_ref.shape
+    kw, width = filt_ref.shape
+    rows = feats_ref.shape[0]
     me = lax.axis_index("atom")
     core = lax.axis_index("wave")
     x = me % side
@@ -99,11 +107,51 @@
     peers = [partner] + [peer for group in ahead for peer in group]
     for peer in peers:
         pl.semaphore_signal(barrier, inc=1, device_id=peer, device_id_type=MESH)
+
+    local = [
+        pltpu.make_async_copy(src, dst, l_sem.at[k])
+        for k, (src, dst) in enumerate(
+            (
+                (mixing_hbm, mixing_ref),
+                (filt_hbm.at[pl.ds(pl.multiple_of(me * kw, kw), kw)], filt_ref),
+                (w_in_hbm, w_in_ref),
+                (w_out_hbm, w_out_ref),
+            )
+        )
+    ]
+    for copy in local:
+        copy.start()
+
+    place = pos_ref[...]
+    high = place.astype(BF).astype(F32)
+    middle = (place - high).astype(BF).astype(F32)
+    stage[...] = jnp.zeros_like(stage)
+    stage[0:3, :rows] = high
+    stage[3:6, :rows] = middle
+    stage[6:9, :rows] = place - high - middle
+    pos_all[0] = stage[:, :rows].astype(BF)
+    slot = lax.broadcasted_iota(jnp.int32, (rows, width), 0)
+    live = slot < counts_ref[0]
+    feats = feats_ref[...].astype(F32)
+    feat_all[0] = jnp.where(live, feats, 0.0).astype(BF)
+
+    window = max(kw, 128)
+    first = pl.multiple_of((me * kw) // window * window, window)
+    shift = me * kw - first
+
+    def turned(raw):
+        for part in range(3):
+            stage[3 * part : 3 * part + 3, :] = raw.astype(F32)
+        found = stage[...]
+        if kw < window:
+            found = pltpu.roll(found, (window - shift) % window, 1)
+        return found.T[:kw].astype(BF)
+
     pl.semaphore_wait(barrier, len(peers))
 
-    def gather(own, store, send, recv):
+    def gather(store, send, recv):
         def copy(src_id, dst_id, peer):
-            src = own if src_id == 0 else store.at[src_id]
+            src = store.at[src_id]
             return pltpu.make_async_remote_copy(
                 src_ref=src,
                 dst_ref=store.at[dst_id],
@@ -136,8 +184,8 @@
 
         return begin, forward, arrive, copies
 
-    p_begin, p_forward, p_arrive, p_copies = gather(pos_ref, pos_all, p_send, p_recv)
-    f_begin, f_forward, f_arrive, f_copies = gather(masked_ref, feat_all, f_send, f_recv)
+    p_begin, p_forward, p_arrive, p_copies = gather(pos_all, p_send, p_recv)
+    f_begin, f_forward, f_arrive, f_copies = gather(feat_all, f_send, f_recv)
 
     def core_copy(src, dst, k):
         return pltpu.make_async_remote_copy(
@@ -150,13 +198,12 @@
         )
 
     p_begin()
-    wave_copy = core_copy(wave_ref, wave_other, 0)
+    wave_copy = core_copy(waves_ref.at[:, pl.ds(first, window)], wave_raw, 0)
     wave_copy.start()
     f_begin()
-    pos_all[0] = pos_ref[...]
-    feat_all[0] = masked_ref[...]
-    mixing_t = mixing_ref[...].T
+    wave_own[...] = turned(waves_ref[:, pl.ds(first, window)])
     wave_copy.wait_recv()
+    wave_other[...] = turned(wave_raw[...])
 
     block = min(kw, 128)
 
@@ -164,12 +211,12 @@
         k = ident(dz, db, dc)
         place = pos_all[k]
         columns = slice(k * rows, (k + 1) * rows)
-        for half, ref in enumerate((wave_ref, wave_other)):
+        for half, ref in enumerate((wave_own, wave_other)):
 
             def one(j, carry):
                 r0 = pl.multiple_of(j * block, block)
                 turns = jnp.dot(
-                    ref[pl.ds(r0, block), :][:, :16], place, preferred_element_type=F32
+                    ref[pl.ds(r0, block), :], place, preferred_element_type=F32
                 )
                 r = turns - jnp.round(turns)
                 zz = r * r
@@ -240,6 +287,9 @@
     sum_copy = core_copy(factors.at[pl.ds(2 * kw, 2 * kw)], factors_in, 1)
     sum_copy.start()
     sums(last, 0, 2 * kw, last == 0)
+    for copy in local:
+        copy.wait()
+    mixing_t = mixing_ref[...].T
     filt = filt_ref[...].astype(F32)
     scale = 1.0 / math.sqrt(atoms_all)
     sum_copy.wait_recv()
@@ -316,14 +366,13 @@
     for dz in range(1, planes):
         mine = mine + received(dz)
 
-    state = masked_ref[...].astype(F32) + mine.T * inv_k
+    state = feats + mine.T * inv_k
     meansq = jnp.mean(state * state, axis=1, keepdims=True)
-    normed = (state * lax.rsqrt(meansq + 1e-06) * gain_ref[...]).astype(BF)
+    normed = (state * lax.rsqrt(meansq + 1e-06) * gain_ref[...].reshape(1, width)).astype(BF)
     inner = jnp.dot(normed, w_in_ref[...], preferred_element_type=F32)
     hidden = (inner / (1.0 + jnp.exp(-inner))).astype(BF)
     result = state + jnp.dot(hidden, w_out_ref[...], preferred_element_type=F32)
-    slot = lax.broadcasted_iota(jnp.int32, (rows, width), 0)
-    out_ref[...] = jnp.where(slot < counts_ref[0], result, 0.0).astype(BF)
+    out_ref[...] = jnp.where(live, result, 0.0)
 
     for copies in (p_copies, f_copies, u_copies):
         for copy in copies.values():
@@ -337,27 +386,28 @@
     planes, side = grid_of(n)
     kwaves_all = waves.shape[1] * cores
     kw = waves.shape[1] // n
-    me = lax.axis_index("atom")
-    live = lax.broadcasted_iota(jnp.int32, (rows, 1), 0) < counts[0]
-    masked = feats * live.astype(BF)
-    high = lax.reduce_precision(positions, 8, 7)
-    rest = positions - high
-    middle = lax.reduce_precision(rest, 8, 7)
-    low = rest - middle
-    pos = jnp.pad(jnp.concatenate([high, middle, low], 0).astype(BF), ((0, 7), (0, 0)))
-    own = lax.dynamic_slice_in_dim(waves, me * kw, kw, 1).astype(BF).T
-    wave = jnp.pad(jnp.concatenate([own, own, own], 1), ((0, 0), (0, 119)))
-    filt = lax.dynamic_slice_in_dim(wave_filter, me * kw, kw, 0)
     vmem = pl.BlockSpec(memory_space=pltpu.VMEM)
+    hbm = pl.BlockSpec(memory_space=pl.ANY)
     return pl.pallas_call(
         functools.partial(kernel, n, planes, side, rows * n * cores, kwaves_all),
-        out_shape=jax.ShapeDtypeStruct((rows, width), BF),
-        in_specs=[pl.BlockSpec(memory_space=pltpu.SMEM)] + [vmem] * 8,
+        out_shape=jax.ShapeDtypeStruct((rows, width), F32),
+        in_specs=[pl.BlockSpec(memory_space=pltpu.SMEM)]
+        + [vmem] * 3
+        + [hbm] * 2
+        + [vmem]
+        + [hbm] * 2,
         out_specs=vmem,
         scratch_shapes=[
+            pltpu.VMEM((kw, width), BF),
+            pltpu.VMEM(mixing.shape, F32),
+            pltpu.VMEM(w_in.shape, BF),
+            pltpu.VMEM(w_out.shape, BF),
+            pltpu.VMEM((16, max(kw, 128)), F32),
+            pltpu.VMEM((kw, 16), BF),
+            pltpu.VMEM((3, max(kw, 128)), waves.dtype),
             pltpu.VMEM((n, 16, rows), BF),
             pltpu.VMEM((n, rows, width), BF),
-            pltpu.VMEM((kw, 128), BF),
+            pltpu.VMEM((kw, 16), BF),
             pltpu.VMEM((4 * kw, n * rows), BF),
             pltpu.VMEM((4 * kw, width), F32),
             pltpu.VMEM((2 * kw, width), F32),
@@ -368,11 +418,12 @@
             pltpu.VMEM((n, width, rows), BF),
         ]
         + [pltpu.SemaphoreType.DMA((n,))] * 6
-        + [pltpu.SemaphoreType.DMA((3,))] * 2,
+        + [pltpu.SemaphoreType.DMA((3,))] * 2
+        + [pltpu.SemaphoreType.DMA((4,))],
         compiler_params=pltpu.CompilerParams(
             collective_id=0, has_side_effects=True, vmem_limit_bytes=60 * 2**20
         ),
-    )(counts, pos, masked, wave, filt, mixing, gain[None, :], w_in, w_out)
+    )(counts, positions, feats, waves, wave_filter, mixing, gain, w_in, w_out).astype(BF)
 
 
 def solution(mesh):

time: 56.9 us -> 51.2 us (0.90)
  local copies, waits for them, and re-layouts: 2.89 us -> 0 us
  other arithmetic: 3.56 us -> 1.54 us
    mul x1 -> x0, other arithmetic: 1.55 us -> none  [body(): masked = feats * live.astype(BF)]
    convert_element_type x1, other arithmetic: 0.01 us -> 1.54 us  [body(): return pl.pallas_call(functools.partial(kernel, n, planes, side, rows * n...]
    unnamed x3 -> x0, local copies, waits for them, and re-layouts: 1.48 us -> none
    transpose x1 -> x0, other arithmetic: 0.7 us -> none  [body(): own = lax.dynamic_slice_in_dim(waves, me * kw, kw, 1).astype(BF).T]
    another operation x1 -> x0, other arithmetic: 0.69 us -> none
    dynamic_slice x1 -> x0, local copies, waits for them, and re-layouts: 0.64 us -> none  [body(): filt = lax.dynamic_slice_in_dim(wave_filter, me * kw, kw, 0)]
    pad x1 -> x0, local copies, waits for them, and re-layouts: 0.63 us -> none  [body(): wave = jnp.pad(jnp.concatenate([own, own, own], 1), ((0, 0), (0, 119)))]
    concatenate x2 -> x0, other arithmetic: 0.61 us -> none  [the longest x1 0.6 us: body(): jnp.concatenate([high, middle, low], 0).astype(BF)]
where the time goes in v2:
time: 51.2 us; the launch traced here: 51.1 us
  Pallas kernels  48.9 us (96%)
  other arithmetic  1.54 us (3%)
  between operations  0.66 us (1%)
    pallas_call x1, Pallas kernels, body(): pl.pallas_call(functools.partial(kernel, n, planes, side, rows * n * core...  48.9 us
    convert_element_type x1, other arithmetic, body(): return pl.pallas_call(functools.partial(kernel, n, planes, side, rows * n...  1.54 us

profile of v2, /device:TPU:0, one launch (start us, length us, event | category | flops | bytes accessed | tf_op | source)
XLA Modules:
  0.0 51.1 jit_solution(16202402237471484129)
XLA Ops:
  0.7 48.9 %shard_map.91 = f32[128,256]{1,0:T(8,128)} custom-call(s32[1]{0:T(128)S(6)} %copy.10.counts_ref, f32[3,128]{1,0:T(4,128)} %pos_ref.1, bf16[128,256]{1,0:T(8,128)(2,1)} %feats_ref.1, s32[3,4096]{1,0:T(4,128)} %waves_ref.1, bf16[4096,256]{1,0:T(8,128)(2,1)} %filt_hbm.1, f32[256,256]{1,0:T(8,128)} %mixing_hbm.1, f32[256]{0:T(256)} %gain_ref.1, ...), custom_call_target="tpu_custom_call" | custom-call | tf_op jit(solution)/shard_map/pallas_call | solution.py:391
  49.5 1.5 %convert_element_type.3 = bf16[128,256]{1,0:T(8,128)(2,1)} convert(f32[128,256]{1,0:T(8,128)} %shard_map.91) | non-fusion elementwise | flops 32768 | bytes 196608 | tf_op jit(solution)/shard_map/convert_element_type | solution.py:426

commit v3 on v2

--- a/solution.py
+++ b/solution.py
@@ -230,7 +230,7 @@
             lax.fori_loop(0, kw // block, one, 0)
 
     group_cols = planes * rows
-    step = min(2 * kw, 256)
+    step = min(kw, 256)
 
     def sums(g, lo, hi, first):
         columns = slice(g * group_cols, (g + 1) * group_cols)
@@ -249,51 +249,69 @@
 
         lax.fori_loop(0, (hi - lo) // step, one, 0)
 
+    groups = side * side
+    near = range(1, side)
+    far = range(1, planes)
+
+    def group_sums(dc, db):
+        g = dc * side + db
+        if g < groups - 1:
+            sums(g, 0, 4 * kw, g == 0)
+
     angles(0, 0, 0)
-    for dz in range(1, planes):
+    for dz in far:
         p_arrive(dz, 0, 0)
         p_forward(dz, 0)
-    for dz in range(1, planes):
-        angles(dz, 0, 0)
+    for db in near:
+        p_arrive(0, db, 0)
+        p_forward(0, db)
+        f_arrive(0, db, 0)
+        f_forward(0, db)
+        angles(0, db, 0)
+    for dz in far:
         f_arrive(dz, 0, 0)
         f_forward(dz, 0)
-    for db in range(1, side):
-        for dz in range(planes):
+        for db in near:
             p_arrive(dz, db, 0)
             p_forward(dz, db)
-    for db in range(1, side):
-        for dz in range(planes):
+        angles(dz, 0, 0)
+    for dz in far:
+        for db in near:
             angles(dz, db, 0)
             f_arrive(dz, db, 0)
             f_forward(dz, db)
-    groups = side * side
-    for g in range(side):
-        if g < groups - 1:
-            sums(g, 0, 4 * kw, g == 0)
-    for dc in range(1, side):
+    for dc in near:
         for db in range(side):
             for dz in range(planes):
                 p_arrive(dz, db, dc)
                 angles(dz, db, dc)
-    for dc in range(1, side):
+            if dc == 1:
+                group_sums(0, db)
+    for dc in near:
         for db in range(side):
             for dz in range(planes):
                 f_arrive(dz, db, dc)
-            g = dc * side + db
-            if g < groups - 1:
-                sums(g, 0, 4 * kw, False)
+            group_sums(dc, db)
     last = groups - 1
-    sums(last, 2 * kw, 4 * kw, last == 0)
-    sum_copy = core_copy(factors.at[pl.ds(2 * kw, 2 * kw)], factors_in, 1)
-    sum_copy.start()
+    sum_copies = []
+    for part in range(2):
+        sums(last, (2 + part) * kw, (3 + part) * kw, last == 0)
+        sum_copies.append(
+            core_copy(
+                factors.at[pl.ds((2 + part) * kw, kw)],
+                factors_in.at[pl.ds(part * kw, kw)],
+                (1, 3)[part],
+            )
+        )
+        sum_copies[part].start()
     sums(last, 0, 2 * kw, last == 0)
     for copy in local:
         copy.wait()
     mixing_t = mixing_ref[...].T
     filt = filt_ref[...].astype(F32)
     scale = 1.0 / math.sqrt(atoms_all)
-    sum_copy.wait_recv()
     for part in range(2):
+        sum_copies[part].wait_recv()
         span = slice(part * kw, (part + 1) * kw)
         total = (factors[span, :] + factors_in[span, :]) * scale * filt
         field_t[:, span] = lax.dot_general(
@@ -329,14 +347,23 @@
         u_copies[k].wait_recv()
         return recv_u[k].astype(F32)
 
-    order = [(dz, db) for db in range(side - 1, -1, -1) for dz in range(planes - 2, -1, -2)]
+    def push(pair, k, dz, dc):
+        for d in range(2):
+            send_u[k + d] = pair[:, d * rows : (d + 1) * rows].astype(BF)
+            if dz + d:
+                start_u(k + d, k + d, back[2][dc - 1])
+
+    order = [
+        (dz, db) for dz in range(planes - 2, -1, -2) for db in range(side - 1, -1, -1)
+    ]
     for dz, db in order:
-        for dc in range(1, side):
+        for dc in near:
             k = ident(dz, db, dc)
-            pair = update_pair(k)
-            for d in range(2):
-                send_u[k + d] = pair[:, d * rows : (d + 1) * rows].astype(BF)
-                start_u(k + d, k + d, back[2][dc - 1])
+            push(update_pair(k), k, dz, dc)
+    for db in range(side - 1, -1, -1):
+        for dc in near:
+            k = ident(0, db, dc)
+            start_u(k, k, back[2][dc - 1])
     for dz, db in order:
         k = ident(dz, db, 0)
         pair = update_pair(k)
@@ -352,16 +379,24 @@
                 acc = acc + received(ident(dz, d, 0))
         return acc
 
-    zorder = [dz + d for dz in range(planes - 2, -1, -2) for d in range(2)]
-    for db in range(side - 1, 0, -1):
-        for dz in zorder:
+    def pass_b(dz):
+        for db in near:
             k = ident(dz, db, 0)
             send_u[k] = collected(dz, db).astype(BF)
             start_u(k, k, back[1][db - 1])
+
+    def pass_a(dz):
+        send_u[dz] = collected(dz, 0).astype(BF)
+        start_u(dz, dz, back[0][dz - 1])
+
+    zorder = [dz + d for dz in range(planes - 2, -1, -2) for d in range(2) if dz + d]
     for dz in zorder:
-        if dz:
-            send_u[dz] = collected(dz, 0).astype(BF)
-            start_u(dz, dz, back[0][dz - 1])
+        pass_b(dz)
+    for dz in zorder[:-1]:
+        pass_a(dz)
+    pass_b(0)
+    if zorder:
+        pass_a(zorder[-1])
     mine = collected(0, 0)
     for dz in range(1, planes):
         mine = mine + received(dz)
@@ -377,7 +412,7 @@
     for copies in (p_copies, f_copies, u_copies):
         for copy in copies.values():
             copy.wait_send()
-    for copy in (wave_copy, sum_copy, field_copy):
+    for copy in (wave_copy, *sum_copies, field_copy):
         copy.wait_send()
 
 
@@ -418,7 +453,7 @@
             pltpu.VMEM((n, width, rows), BF),
         ]
         + [pltpu.SemaphoreType.DMA((n,))] * 6
-        + [pltpu.SemaphoreType.DMA((3,))] * 2
+        + [pltpu.SemaphoreType.DMA((4,))] * 2
         + [pltpu.SemaphoreType.DMA((4,))],
         compiler_params=pltpu.CompilerParams(
             collective_id=0, has_side_effects=True, vmem_limit_bytes=60 * 2**20

time: 51.2 us -> 51 us (level)
  no operation moved by 1% of the time
where the time goes in v3:
time: 51 us; the launch traced here: 50.8 us
  Pallas kernels  48.6 us (95%)
  other arithmetic  1.54 us (3%)
  between operations  0.66 us (1%)
    pallas_call x1, Pallas kernels, body(): pl.pallas_call(functools.partial(kernel, n, planes, side, rows * n * core...  48.6 us
    convert_element_type x1, other arithmetic, body(): return pl.pallas_call(functools.partial(kernel, n, planes, side, rows * n...  1.54 us

profile of v3, /device:TPU:0, one launch (start us, length us, event | category | flops | bytes accessed | tf_op | source)
XLA Modules:
  0.0 50.8 jit_solution(13362627082124734096)
XLA Ops:
  0.7 48.6 %shard_map.91 = f32[128,256]{1,0:T(8,128)} custom-call(s32[1]{0:T(128)S(6)} %copy.10.counts_ref, f32[3,128]{1,0:T(4,128)} %pos_ref.1, bf16[128,256]{1,0:T(8,128)(2,1)} %feats_ref.1, s32[3,4096]{1,0:T(4,128)} %waves_ref.1, bf16[4096,256]{1,0:T(8,128)(2,1)} %filt_hbm.1, f32[256,256]{1,0:T(8,128)} %mixing_hbm.1, f32[256]{0:T(256)} %gain_ref.1, ...), custom_call_target="tpu_custom_call" | custom-call | tf_op jit(solution)/shard_map/pallas_call | solution.py:426
  49.3 1.5 %convert_element_type.3 = bf16[128,256]{1,0:T(8,128)(2,1)} convert(f32[128,256]{1,0:T(8,128)} %shard_map.91) | non-fusion elementwise | flops 32768 | bytes 196608 | tf_op jit(solution)/shard_map/convert_element_type | solution.py:461
